TPU v7x, 128 devices: a whole 4x4x4 slice. The times are simulated.
128 devices in a mesh: blk: 16 (over z, y), beam: 8 (over x, core).
Axes of the slice: x: 4, y: 4, z: 4, core: 2. Of those that a mesh axis runs over, the one named last changes fastest.
Arguments:
- sky_coefficients: bfloat16 [2, 128, 3, 2, 32, 4096], P(None, None, None, None, 'blk'), may hold values from -6 to 6
- beam_window: bfloat16 [2, 16, 4096], P(None, 'beam'), may hold values from -5 to 5
- legendre: bfloat16 [32, 2, 4096, 256], P('blk'), as said below
- azimuth_modes: int32 [32], P('blk'), may hold values from 0 to 8191, as said below
- orientation: float32 [128, 16, 512], P('beam'), may hold values from -1 to 1
Outputs:
- sky_map: bfloat16 [128, 3, 512, 128], P('beam', None, 'blk')
Inputs may be any that keep to these rules, and one draw needn't show every extreme that they name: `azimuth_modes`: distinct values; 0 and 8191 are always among them. legendre[m, p, i, t] is zero wherever 2 * i + p < azimuth_modes[m].
All inputs are finite; a program needn't handle non-finite values.
Results may differ from a plain program's by a relative error of at most 0.0049.
Values may be sent and summed in bfloat16 or wider, within the bound.
No kernel may reach another device: no remote copies, remote signals or barrier semaphores. Data moves between devices by JAX's collectives and lax.ppermute only.
A program may use at most 256 MiB of HBM per device.

v0:
```python
import math

import jax
import jax.numpy as jnp
from jax import lax
from jax.sharding import PartitionSpec as P

LMAX = 8192
NPHI = 128


def basis_table(azimuth_modes):
    column = jnp.arange(NPHI, dtype=jnp.int32)
    phase = (azimuth_modes[:, None] * column[None, :] % (2 * LMAX)).astype(jnp.float32) * (
        math.pi / LMAX
    )
    weight = jnp.where(azimuth_modes == 0, 1.0, 2.0).astype(jnp.float32)[:, None]
    return jnp.stack([weight * jnp.cos(phase), -weight * jnp.sin(phase)])


def beam_reduce(values):
    return lax.psum_scatter(values, "beam", scatter_dimension=1, tiled=True)


def orient_sum(values, weights):
    by_component = jnp.swapaxes(weights, 0, 1)
    return jnp.sum(values * by_component[None, :, :, None, None, :], axis=1)


def shards(sky_coefficients, beam_window, legendre, azimuth_modes, orientation):
    half = sky_coefficients.shape[5]
    north_count = legendre.shape[3]
    local_modes = legendre.shape[0]
    turn_weights = lax.all_to_all(orientation, "beam", split_axis=1, concat_axis=0, tiled=True)
    nsims = sky_coefficients.shape[1]
    components = beam_window.shape[1]
    row_count = components * nsims * 3 * 2
    slabs = []
    for slot in range(local_modes):
        coef = sky_coefficients[:, :, :, :, slot]
        table = legendre[slot]
        mode = azimuth_modes[slot]

        def accumulate(start, width, carry, coef=coef, table=table):
            weighted = (
                beam_window[:, :, None, None, None, :].astype(jnp.float32)
                * coef[:, None, :, :, :, :].astype(jnp.float32)
            ).astype(jnp.bfloat16)
            weighted = weighted.reshape(2, row_count, width)
            parts = lax.dot_general(
                weighted, table, (((2,), (1,)), ((0,), (0,))), preferred_element_type=jnp.float32
            )
            return (parts[0], parts[1])

        zeros = jnp.zeros((row_count, north_count), jnp.float32)
        carry = accumulate(0, half, (zeros, zeros))
        parity_sign = jnp.where(mode % 2 == 0, 1.0, -1.0).astype(jnp.float32)
        north_cycles = carry[0] + carry[1]
        south_cycles = parity_sign * (carry[0] - carry[1])
        slabs.append(jnp.concatenate([north_cycles, jnp.flip(south_cycles, 1)], 1))
    cycle_values = jnp.stack(slabs)
    modes_all = lax.all_gather(azimuth_modes, "blk", axis=0, tiled=True)
    basis = basis_table(modes_all)
    moved = lax.all_to_all(cycle_values, "blk", split_axis=2, concat_axis=0, tiled=True)
    span = moved.shape[2]
    shaped = moved.reshape(moved.shape[0], components, nsims, 3, 2, span)
    cycle_weights = lax.dynamic_slice_in_dim(turn_weights, lax.axis_index("blk") * span, span, 2)
    oriented = orient_sum(shaped, cycle_weights)
    local_cycles = beam_reduce(oriented)
    result = jnp.einsum("mscrt,rmj->sctj", local_cycles, basis, precision=lax.Precision.HIGHEST)
    return result.astype(jnp.bfloat16)


def solution(mesh):
    placed = (
        P(None, None, None, None, "blk", None),
        P(None, "beam", None),
        P("blk", None, None, None),
        P("blk"),
        P("beam", None, None),
    )
    return jax.shard_map(
        shards, mesh=mesh, in_specs=placed, out_specs=P("beam", None, "blk", None), check_vma=False
    )
```

profile of v0, /device:TPU:1, one launch (start us, length us, event | category | flops | bytes accessed | tf_op | source)
XLA Modules:
  0.0 666.5 jit_solution(16141251154845750858)
XLA Ops:
  6.5 2.2 copy.43
  8.7 5.8 all-to-all-start.1
  14.5 1.3 fusion.20
  19.7 80.8 %fusion.19 = (bf16[2,128,3,2,1,4096]{5,4,3,2,1,0:T(2,128)(2,1)}, bf16[2,128,3,2,1,4096]{5,4,3,2,1,0:T(2,128)(2,1)}) fusion(bf16[2,128,3,2,2,4096]{5,4,3,2,1,0:T(2,128)(2,1)} %param.5), kind=kLoop, calls=%fused_computation.42 | loop fusion | bytes 50331648 | tf_op jit(solution)/shard_map/slice | solution.py:40
  100.5 59.7 %fusion = (f32[2,128,3,2,4096]{4,1,3,2,0:T(8,128)}, f32[2,128,3,2,4096]{4,1,3,2,0:T(8,128)}) fusion(bf16[2,128,3,2,1,4096]{5,4,3,2,1,0:T(2,128)(2,1)} %get-tuple-element.6, bf16[2,128,3,2,1,4096]{5,4,3,2,1,0:T(2,128)(2,1)} %get-tuple-element.5), kind=kLoop, calls=%fused_computation.4 | loop fusion | flops 12582912 | bytes 75497472 | tf_op jit(solution)/shard_map/convert_element_type | solution.py:47
  160.3 42.3 %copy.36 = f32[2,128,3,2,4096]{4,3,2,1,0:T(2,128)} copy(f32[2,128,3,2,4096]{4,1,3,2,0:T(8,128)} %get-tuple-element.20) | data formatting | bytes 50331648 | tf_op jit(solution)/shard_map/convert_element_type | solution.py:47
  202.6 42.1 %copy.39 = f32[2,128,3,2,4096]{4,3,2,1,0:T(2,128)} copy(f32[2,128,3,2,4096]{4,1,3,2,0:T(8,128)} %get-tuple-element.19) | data formatting | bytes 50331648 | tf_op jit(solution)/shard_map/convert_element_type | solution.py:47
  244.7 37.4 %multiply_convert_fusion.1 = (bf16[2,2,128,3,2,4096]{5,4,3,2,1,0:T(2,128)(2,1)}, bf16[2,2,128,3,2,4096]{5,4,3,2,1,0:T(2,128)(2,1)}) fusion(f32[2,128,3,2,4096]{4,3,2,1,0:T(2,128)} %copy.36, f32[2,2,4096]{2,1,0:T(2,128)S(1)} %convert_element_type.58, f32[2,128,3,2,4096]{4,3,2,1,0:T(2,128)} %copy.39), kind=kLoop, calls=%fused_computation.1 | loop fusion | flops 50331648 | bytes 100728832 | tf_op jit(solution)/shard_map/convert_element_type | solution.py:48
  282.0 36.7 %convert_element_type.66 = bf16[2,1536,4096]{2,1,0:T(8,128)(2,1)} reshape(bf16[2,2,128,3,2,4096]{5,4,3,2,1,0:T(2,128)(2,1)} %get-tuple-element.12) | data formatting | bytes 50331648 | tf_op jit(solution)/shard_map/convert_element_type | solution.py:48
  318.7 14.4 %fusion.2 = f32[2,1536,256]{1,2,0:T(8,128)} fusion(bf16[2,1536,4096]{2,1,0:T(8,128)(2,1)} %convert_element_type.66, bf16[2,2,4096,256]{3,2,1,0:T(8,128)(2,1)} %param.7), kind=kOutput, calls=%fused_computation.8 | convolution fusion | flops 6442450944 | bytes 32505856 | tf_op jit(solution)/shard_map/dot_general | solution.py:50
  333.1 3.3 add_bitcast_fusion
  336.4 0.8 reverse.7
  337.2 36.7 %convert_element_type.62 = bf16[2,1536,4096]{2,1,0:T(8,128)(2,1)} reshape(bf16[2,2,128,3,2,4096]{5,4,3,2,1,0:T(2,128)(2,1)} %get-tuple-element.11) | data formatting | bytes 50331648 | tf_op jit(solution)/shard_map/convert_element_type | solution.py:48
  373.9 14.6 %fusion.4 = f32[2,1536,256]{1,2,0:T(8,128)} fusion(bf16[2,1536,4096]{2,1,0:T(8,128)(2,1)} %convert_element_type.62, bf16[2,2,4096,256]{3,2,1,0:T(8,128)(2,1)} %param.7), kind=kOutput, calls=%fused_computation.10 | convolution fusion | flops 6442450944 | bytes 32505856 | tf_op jit(solution)/shard_map/dot_general | solution.py:50
  388.5 3.8 add_bitcast_fusion.1
  392.3 10.3 %reverse.6 = f32[1536,256]{0,1:T(8,128)S(1)} reverse(f32[1536,256]{0,1:T(8,128)} %get-tuple-element.8), dimensions={1} | reverse | bytes 3145728 | tf_op jit(solution)/shard_map/reverse
  402.7 1.7 maximum_bitcast_fusion.1
  404.6 0.2 maximum_bitcast_fusion
  404.8 0.4 pad_maximum_fusion
  405.2 7.5 %copy.41 = f32[2,1536,512]{1,0,2:T(2,128)} copy(f32[2,1536,512]{1,2,0:T(8,128)S(1)} %pad_maximum_fusion) | data formatting | bytes 12582912 | tf_op jit(solution)/shard_map/stack | solution.py:61
  412.8 7.8 %all-to-all-start = ((f32[2,1536,512]{1,0,2:T(2,128)}), f32[2,1536,512]{1,0,2:T(2,128)}, u32[]{:S(2)}, u32[]{:S(2)}) async-start(f32[2,1536,512]{1,0,2:T(2,128)} %copy.41), calls=%async_computation | async-start | bytes 12582912 | tf_op jit(solution)/shard_map/all_to_all | solution.py:64
  420.6 1.1 copy.44
  421.8 93.6 %all-to-all-done = f32[2,1536,512]{1,0,2:T(2,128)} async-done(((f32[2,1536,512]{1,0,2:T(2,128)}), f32[2,1536,512]{1,0,2:T(2,128)}, u32[]{:S(2)}, u32[]{:S(2)}) %all-to-all-start) | async-done | bytes 6291488 | tf_op jit(solution)/shard_map/all_to_all | solution.py:64
  515.4 17.2 %copy.42 = f32[2,1536,16,32]{3,1,0,2:T(8,128)} copy(f32[2,1536,16,32]{1,0,3,2:T(2,128)} %bitcast.12) | data formatting | bytes 12582912 | tf_op jit(solution)/shard_map/all_to_all | solution.py:64
  532.6 34.5 %multiply_reduce_fusion = f32[32,128,3,2,32]{4,3,2,1,0:T(2,128)} fusion(f32[32,2,128,3,2,32]{5,4,3,2,1,0:T(2,128)} %bitcast.56, f32[2,128,32]{2,1,0:T(8,128)S(1)} %dynamic-slice_bitcast_fusion), kind=kLoop, calls=%fused_computation.2 | loop fusion | flops 2359296 | bytes 9469952 | tf_op jit(solution)/shard_map/reduce_sum | solution.py:27
  567.1 16.4 %copy.45 = f32[32,128,3,2,32]{4,0,3,2,1:T(8,128)} copy(f32[32,128,3,2,32]{4,3,2,1,0:T(2,128)} %multiply_reduce_fusion) | data formatting | bytes 6291456 | tf_op jit(solution)/shard_map/reduce_sum | solution.py:27
  583.6 0.6 copy-done.3
  584.2 0.6 dynamic-slice
  585.4 0.2 dynamic-update-slice
  585.7 9.4 %all-reduce = s32[32]{0:T(128)S(1)} all-reduce(s32[32]{0:T(128)S(1)} %dynamic-update-slice), channel_id=1, replica_groups=mesh['blk'=16,'beam'=8] {'blk'}, use_global_device_ids=true, to_apply=%add | all-reduce | flops 32 | bytes 256
  595.2 59.2 %reduce-scatter.2.cloned.1.call-done = f32[32,16,3,2,32]{4,0,3,2,1:T(8,128)} async-done(((f32[32,128,3,2,32]{4,0,3,2,1:T(8,128)}), f32[32,16,3,2,32]{4,0,3,2,1:T(8,128)}) %reduce-scatter.2.cloned.1.call-update) | async-done | bytes 393232 | tf_op jit(solution)/shard_map/reduce_scatter | solution.py:22
  654.4 4.8 fusion.8
  (17 shorter events, 0.6 us)
Async XLA Ops:
  8.7 404.0 %all-to-all-start.1 = ((f32[16,16,512]{2,0,1:T(8,128)}), f32[16,16,512]{2,0,1:T(8,128)}, u32[]{:S(2)}, u32[]{:S(2)}) async-start(f32[16,16,512]{2,0,1:T(8,128)} %copy.43), calls=%async_computation.1 | async-start | bytes 1048576 | tf_op jit(solution)/shard_map/all_to_all | solution.py:34
  160.3 42.3 %copy-start.1 = (bf16[2,2,4096]{2,1,0:T(2,128)(2,1)S(1)}, bf16[2,2,4096]{2,1,0:T(2,128)(2,1)}, u32[]{:S(2)}) copy-start(bf16[2,2,4096]{2,1,0:T(2,128)(2,1)} %param.6) | copy-start | bytes 98308
  402.6 2.0 copy-start
  412.8 102.7 %all-to-all-start = ((f32[2,1536,512]{1,0,2:T(2,128)}), f32[2,1536,512]{1,0,2:T(2,128)}, u32[]{:S(2)}, u32[]{:S(2)}) async-start(f32[2,1536,512]{1,0,2:T(2,128)} %copy.41), calls=%async_computation | async-start | bytes 12582912 | tf_op jit(solution)/shard_map/all_to_all | solution.py:64
  420.6 233.8 %reduce-scatter.2.cloned.1.call-start = ((), (), s32[]{:S(2)}) async-start(), calls=%async_computation.3 | async-start | bytes 14155776 | tf_op jit(solution)/shard_map/reduce_scatter | solution.py:22
  583.5 0.7 copy-start.3
  583.5 1.9 copy-start.2
Sparse Core Ops, SparseCore 0:
  583.7 70.7 reduce-scatter.1
where the time goes:
time: 678 us; the launch traced here: 666 us
  local copies, waits for them, and re-layouts  297 us (44%)
  waiting for transfers between devices  153 us (23%)
  other arithmetic  141 us (21%)
  matrix products  33.8 us (5%)
  between operations  18.5 us (3%)
  starting transfers between devices  13.6 us (2%)
  blocking collectives  9.4 us (1%)
    all_to_all x1, waiting for transfers between devices, shards(): lax.all_to_all(cycle_values, 'blk', split_axis=2, concat_axis=0, tiled=True)  93.6 us
    convert_element_type x2, local copies, waits for them, and re-layouts, accumulate(): coef[:, None, :, :, :, :].astype(jnp.float32)  84.4 us
    slice x1, local copies, waits for them, and re-layouts, shards(): coef = sky_coefficients[:, :, :, :, slot]  80.8 us
    convert_element_type x2, local copies, waits for them, and re-layouts, accumulate(): weighted = (beam_window[:, :, None, None, None, :].astype(jnp.float32) *...  73.3 us
    convert_element_type x1, other arithmetic, accumulate(): coef[:, None, :, :, :, :].astype(jnp.float32)  59.7 us
    reduce_scatter x1, waiting for transfers between devices, beam_reduce(): return lax.psum_scatter(values, 'beam', scatter_dimension=1, tiled=True)  59.2 us
    convert_element_type x1, other arithmetic, accumulate(): weighted = (beam_window[:, :, None, None, None, :].astype(jnp.float32) *...  37.4 us
    reduce_sum x1, other arithmetic, orient_sum(): return jnp.sum(values * by_component[None, :, :, None, None, :], axis=1)  34.5 us
  transfers between devices with their start and end apart: 3, of which 2 were waited for; matrix products, arithmetic and copies ran while one was open for 59% of the time, Pallas kernels for 0%

commit v1 on v0

v1 whole, which is shorter than its diff:
```python
import functools
import math

import jax
import jax.numpy as jnp
from jax import lax
from jax.experimental import pallas as pl
from jax.experimental.pallas import tpu as pltpu
from jax.sharding import PartitionSpec as P

LMAX = 8192
NPHI = 128
CHUNK = 512
BF = jnp.bfloat16
F32 = jnp.float32


def synth_kernel(modes, coef, window, table, weights, out, leg, acc, lhs, win32, sems):
    rows, half = coef.shape[2], coef.shape[3]
    chunks = half // CHUNK
    comps = 2 * window.shape[0]

    def first(slot, p):
        return jnp.minimum((modes[slot] - p + 1) // 2 // CHUNK, chunks - 1)

    def copy(slot, p, c):
        at = pl.ds(pl.multiple_of(c * CHUNK, CHUNK), CHUNK)
        return pltpu.make_async_copy(table.at[slot, p, at, :], leg.at[slot, p, at, :], sems.at[slot, p, c])

    for slot in range(2):
        for p in range(2):
            lax.fori_loop(first(slot, p), chunks, lambda c, _: (copy(slot, p, c).start(), 0)[1], 0)

    for src in range(window.shape[0]):
        for p in range(2):
            win32[p, pl.ds(2 * src, 2), :] = window[src, p].astype(F32)

    def step(slot, p, c):
        copy(slot, p, c).wait()
        at = pl.ds(pl.multiple_of(c * CHUNK, CHUNK), CHUNK)
        sky = coef[slot, p, :, at]
        for k in range(comps):
            gain = jnp.broadcast_to(win32[p, pl.ds(k, 1), at], (rows, CHUNK)).astype(BF)
            lhs[pl.ds(k * rows, rows), :] = sky * gain
        return jnp.dot(lhs[...], leg[slot, p, at, :], preferred_element_type=F32)

    lane = lax.broadcasted_iota(jnp.int32, (256, 256), 0)
    flip = jnp.where(lane + lax.broadcasted_iota(jnp.int32, (256, 256), 1) == 255, 1.0, 0.0).astype(BF)
    group = lax.broadcasted_iota(jnp.int32, (24, 128), 1) // 32
    for slot in range(2):
        for p in range(2):
            acc[p] = jnp.zeros(acc.shape[1:], F32)

            def body(c, _, slot=slot, p=p):
                acc[p] = acc[p] + step(slot, p, c)
                return 0

            lax.fori_loop(first(slot, p), chunks, body, 0)
        sign = jnp.where(modes[slot] % 2 == 0, 1.0, -1.0).astype(F32)
        north, south = [], []
        for b in range(4):
            for c in range(3):
                row = b * 24 + c * 8
                n = jnp.zeros((8, 256), F32)
                s = jnp.zeros((8, 256), F32)
                for k in range(comps):
                    even = acc[0, pl.ds(k * rows + row, 8), :]
                    odd = acc[1, pl.ds(k * rows + row, 8), :]
                    n = n + (even + odd) * weights[k, b, :, pl.ds(0, 256)]
                    s = s + (even - odd) * weights[k, b, :, pl.ds(256, 256)]
                north.append(n)
                south.append(s * sign)
        north = jnp.concatenate(north, 0)
        south = jnp.dot(jnp.concatenate(south, 0).astype(BF), flip, preferred_element_type=F32)
        for tile in range(4):
            half_map = north if tile < 2 else south
            part = half_map[:, (tile % 2) * 128:(tile % 2) * 128 + 128]
            for g in range(4):
                send = jnp.zeros((24, 128), F32)
                for b in range(4):
                    piece = part[b * 24:(b + 1) * 24]
                    if b != g:
                        piece = pltpu.roll(piece, ((b - g) * 32) % 128, 1)
                    send = jnp.where(group == b, piece, send)
                out[tile * 4 + g, pl.ds(slot * 24, 24), :] = send.astype(BF)
    sub = lax.broadcasted_iota(jnp.int32, (8, 128), 0)
    tail = jnp.zeros((8, 128), jnp.int32)
    for slot in range(2):
        tail = jnp.where(sub == 2 * slot, modes[slot] // 128, tail)
        tail = jnp.where(sub == 2 * slot + 1, modes[slot] % 128, tail)
    tail = tail.astype(F32).astype(BF)
    for dst in range(16):
        out[dst, pl.ds(48, 8), :] = tail


def synth(modes, coef, window, table, weights):
    half = coef.shape[3]
    rows = 2 * window.shape[0] * coef.shape[2]
    vm = pl.BlockSpec(memory_space=pltpu.VMEM)
    return pl.pallas_call(
        synth_kernel,
        out_shape=jax.ShapeDtypeStruct((16, 56, 128), BF),
        in_specs=[pl.BlockSpec(memory_space=pltpu.SMEM), vm, vm, pl.BlockSpec(memory_space=pl.ANY), vm],
        out_specs=vm,
        scratch_shapes=[
            pltpu.VMEM((2, 2, half, 256), BF),
            pltpu.VMEM((2, rows, 256), F32),
            pltpu.VMEM((rows, CHUNK), BF),
            pltpu.VMEM((2, 2 * window.shape[0], half), F32),
            pltpu.SemaphoreType.DMA((2, 2, half // CHUNK)),
        ],
        name="synth",
    )(modes, coef, window, table, weights)


def map_kernel(got, out, wide):
    wide[...] = got[...].reshape(wide.shape).astype(F32)

    def take(row):
        return wide[pl.ds(row, 16, stride=56), :]

    column = lax.broadcasted_iota(jnp.int32, (16, 128), 1)
    cosines, sines = [], []
    for slot in range(2):
        mode = (take(48 + 2 * slot) * 128.0 + take(49 + 2 * slot)).astype(jnp.int32)
        phase = ((mode * column) % (2 * LMAX)).astype(F32) * (math.pi / LMAX)
        weight = jnp.where(mode == 0, 1.0, 2.0)
        cosines.append(weight * jnp.cos(phase))
        sines.append(-weight * jnp.sin(phase))
    basis = jnp.concatenate(cosines + sines, 0)
    high = basis.astype(BF)
    low = (basis - high.astype(F32)).astype(BF)
    basis = jnp.concatenate([high, low], 0)
    for c in range(3):
        for a in range(4):
            x = jnp.concatenate([take(slot * 24 + c * 8 + r * 4 + a) for r in range(2) for slot in range(2)], 0)
            x = x.T.astype(BF)
            y = jnp.dot(jnp.concatenate([x, x], 1), basis, preferred_element_type=F32)
            for b in range(4):
                out[4 * a + b, c] = y[b * 32:(b + 1) * 32].astype(BF)


def to_map(got):
    vm = pl.BlockSpec(memory_space=pltpu.VMEM)
    return pl.pallas_call(
        map_kernel,
        out_shape=jax.ShapeDtypeStruct((16, 3, 32, NPHI), BF),
        in_specs=[vm],
        out_specs=vm,
        scratch_shapes=[pltpu.VMEM((16 * 56, 128), F32)],
        name="to_map",
    )(got)


def shards(sky_coefficients, beam_window, legendre, azimuth_modes, orientation):
    half = sky_coefficients.shape[5]
    me = lax.axis_index("beam")
    window = lax.all_to_all(
        jnp.broadcast_to(beam_window[None], (8,) + beam_window.shape), "beam", 0, 0, tiled=True
    )
    coef = lax.dynamic_slice_in_dim(sky_coefficients, me * 16, 16, 1)
    coef = coef.reshape(2, 4, 4, 3, 2, 2, half).transpose(5, 0, 2, 3, 4, 1, 6).reshape(2, 2, 96, half)
    weights = orientation.transpose(1, 0, 2).reshape(16, 4, 1, 4, 512).transpose(0, 3, 2, 1, 4)
    weights = jnp.concatenate([weights[..., :256], jnp.flip(weights[..., 256:], -1)], -1)
    weights = jnp.broadcast_to(weights, (16, 4, 2, 4, 512)).reshape(16, 4, 8, 512)
    sent = synth(azimuth_modes, coef, window, legendre, weights)
    got = lax.all_to_all(sent, "blk", 0, 0, tiled=True)
    return to_map(got)


def solution(mesh):
    placed = (
        P(None, None, None, None, "blk", None),
        P(None, "beam", None),
        P("blk", None, None, None),
        P("blk"),
        P("beam", None, None),
    )
    return jax.shard_map(
        shards, mesh=mesh, in_specs=placed, out_specs=P("beam", None, "blk", None), check_vma=False
    )
```

time: 678 us -> 67.9 us (0.10); the launches traced: 666 us -> 67.8 us
  local copies, waits for them, and re-layouts: 297 us -> 17.2 us
  waiting for transfers between devices: 153 us -> 0.01 us
  other arithmetic: 141 us -> 1 us
  matrix products: 33.8 us -> 0 us
  blocking collectives: 9.4 us -> 28.9 us
  between operations: 18.5 us -> 0.07 us
  Pallas kernels: 0 us -> 14.8 us
  starting transfers between devices: 13.6 us -> 5.79 us
    convert_element_type x4 -> x0, local copies, waits for them, and re-layouts: 158 us -> none  [the longest x2 84.4 us: accumulate(): coef[:, None, :, :, :, :].astype(jnp.float32)]
    convert_element_type x3 -> x0, other arithmetic: 97.1 us -> none  [the longest x1 59.7 us: accumulate(): coef[:, None, :, :, :, :].astype(jnp.float32)]
    all_to_all x2 -> x1, waiting for transfers between devices: 93.6 us -> 0.01 us  [shards(): lax.all_to_all(jnp.broadcast_to(beam_window[None], (8,) + beam_window.sha...]
    slice x2 -> x1, local copies, waits for them, and re-layouts: 82.2 us -> 0.86 us  [shards(): weights[..., :256]]
    reduce_scatter x1 -> x0, waiting for transfers between devices: 59.2 us -> none  [beam_reduce(): return lax.psum_scatter(values, 'beam', scatter_dimension=1, tiled=True)]
    reduce_sum x1 -> x0, other arithmetic: 34.5 us -> none  [orient_sum(): return jnp.sum(values * by_component[None, :, :, None, None, :], axis=1)]
    dot_general x3 -> x0, matrix products: 33.8 us -> none  [the longest x2 29 us: accumulate(): lax.dot_general(weighted, table, (((2,), (1,)), ((0,), (0,))), preferred_...]
    all_to_all x0 -> x1, blocking collectives: none -> 28.9 us  [shards(): got = lax.all_to_all(sent, 'blk', 0, 0, tiled=True)]
  transfers between devices with their start and end apart: 3 -> 1, of which waited for: 2 -> 0; matrix products, arithmetic and copies ran while one was open for 59% -> 23% of each run, Pallas kernels for 0% -> 0%
where the time goes in v1:
time: 67.9 us; the launch traced here: 67.8 us
  blocking collectives  28.9 us (43%)
  local copies, waits for them, and re-layouts  17.2 us (25%)
  Pallas kernels  14.8 us (22%)
  starting transfers between devices  5.79 us (9%)
  other arithmetic  1 us (1%)
    all_to_all x1, blocking collectives, shards(): got = lax.all_to_all(sent, 'blk', 0, 0, tiled=True)  28.9 us
    pallas_call x1, Pallas kernels, synth(): pl.pallas_call(synth_kernel, out_shape=jax.ShapeDtypeStruct((16, 56, 128)...  12.5 us
    all_to_all x1, starting transfers between devices, shards(): lax.all_to_all(jnp.broadcast_to(beam_window[None], (8,) + beam_window.sha...  5.79 us
    dynamic_slice x1, local copies, waits for them, and re-layouts, shards(): coef = lax.dynamic_slice_in_dim(sky_coefficients, me * 16, 16, 1)  5 us
    transpose x1, local copies, waits for them, and re-layouts, shards(): coef.reshape(2, 4, 4, 3, 2, 2, half).transpose(5, 0, 2, 3, 4, 1, 6)  3.04 us
    reshape x1, local copies, waits for them, and re-layouts, shards(): coef.reshape(2, 4, 4, 3, 2, 2, half).transpose(5, 0, 2, 3, 4, 1, 6)  2.99 us
    pallas_call x1, Pallas kernels, to_map(): pl.pallas_call(map_kernel, out_shape=jax.ShapeDtypeStruct((16, 3, 32, NPH...  2.24 us
    broadcast_in_dim x1, local copies, waits for them, and re-layouts, shards(): jnp.broadcast_to(beam_window[None], (8,) + beam_window.shape)  1.66 us
  transfers between devices with their start and end apart: 1, of which 0 were waited for; matrix products, arithmetic and copies ran while one was open for 23% of the time, Pallas kernels for 0%

profile of v1, /device:TPU:1, one launch (start us, length us, event | category | flops | bytes accessed | tf_op | source)
XLA Modules:
  0.0 67.8 jit_solution(12259726025887627473)
XLA Ops:
  0.0 1.7 %broadcast_in_dim.6 = bf16[8,2,2,4096]{3,2,1,0:T(2,128)(2,1)} broadcast(bf16[2,2,4096]{2,1,0:T(2,128)(2,1)} %param.6), dimensions={1,2,3} | broadcast | bytes 294912 | tf_op jit(solution)/shard_map/broadcast_in_dim | solution.py:159
  1.7 5.8 %all-to-all-start = ((bf16[8,2,2,4096]{3,2,1,0:T(2,128)(2,1)}), bf16[8,2,2,4096]{3,2,1,0:T(2,128)(2,1)S(1)}, u32[]{:S(2)}, u32[]{:S(2)}) async-start(bf16[8,2,2,4096]{3,2,1,0:T(2,128)(2,1)} %broadcast_in_dim.6), calls=%async_computation | async-start | bytes 524288 | tf_op jit(solution)/shard_map/all_to_all | solution.py:158
  7.5 0.0 copy-start.1
  7.5 5.0 %constant_dynamic-slice_fusion = bf16[2,16,3,2,2,4096]{5,4,3,2,1,0:T(2,128)(2,1)S(1)} fusion(bf16[2,128,3,2,2,4096]{5,4,3,2,1,0:T(2,128)(2,1)} %param.5, s32[]{:T(128)S(6)} %select_n.3), kind=kLoop, calls=%fused_computation.1 | loop fusion | bytes 6291460 | tf_op jit(solution)/shard_map/dynamic_slice | solution.py:161
  12.5 0.0 copy-done.1
  12.5 0.9 %fusion = (f32[16,4,1,4,256]{4,0,1,3,2:T(8,128)}, f32[16,4,1,4,256]{4,0,1,3,2:T(8,128)}) fusion(f32[16,4,1,4,512]{4,0,1,3,2:T(8,128)S(1)} %bitcast.11), kind=kLoop, calls=%fused_computation.2 | loop fusion | bytes 1048576 | tf_op jit(solution)/shard_map/slice | solution.py:164
  13.3 3.0 %copy.7 = bf16[2,2,4,3,2,4,4096]{6,5,4,3,2,1,0:T(4,128)(2,1)S(1)} copy(bf16[2,2,4,3,2,4,4096]{6,0,4,3,2,5,1:T(2,128)(2,1)S(1)} %bitcast.10) | data formatting | bytes 6291456 | tf_op jit(solution)/shard_map/transpose | solution.py:162
  16.4 3.0 %reshape.14.coef = bf16[2,2,96,4096]{3,2,1,0:T(8,128)(2,1)} reshape(bf16[2,2,4,3,2,4,4096]{6,5,4,3,2,1,0:T(4,128)(2,1)S(1)} %copy.7) | data formatting | bytes 6291456 | tf_op jit(solution)/shard_map/reshape | solution.py:162
  19.4 1.1 %rev.4 = f32[16,4,1,4,256]{4,0,1,3,2:T(8,128)S(1)} reverse(f32[16,4,1,4,256]{4,0,1,3,2:T(8,128)} %get-tuple-element.6), dimensions={4} | reverse | bytes 524288 | tf_op jit(solution)/shard_map/jit(_flip)/rev | solution.py:164
  20.5 1.0 %maximum_bitcast_fusion = f32[16,4,4,512]{3,0,1,2:T(8,128)S(1)} fusion(f32[16,4,1,4,256]{4,0,1,3,2:T(8,128)S(1)} %rev.4, f32[16,4,1,4,256]{4,0,1,3,2:T(8,128)} %get-tuple-element.5), kind=kLoop, calls=%fused_computation | loop fusion | flops 131072 | bytes 1048576 | tf_op jit(solution)/shard_map/broadcast_in_dim | solution.py:165
  21.5 0.3 copy.8
  21.9 0.2 broadcast_in_dim.15
  22.0 1.3 %reshape.16.weights = f32[16,4,8,512]{3,2,1,0:T(8,128)} reshape(f32[16,4,2,4,512]{4,3,2,1,0:T(4,128)S(1)} %broadcast_in_dim.15) | data formatting | bytes 2097152 | tf_op jit(solution)/shard_map/reshape | solution.py:165
  23.4 0.0 all-to-all-done.window
  23.4 0.0 copy-start
  23.4 0.7 %copy-done = bf16[8,2,2,4096]{3,2,1,0:T(2,128)(2,1)} copy-done((bf16[8,2,2,4096]{3,2,1,0:T(2,128)(2,1)}, bf16[8,2,2,4096]{3,2,1,0:T(2,128)(2,1)S(1)}, u32[]{:S(2)}) %copy-start) | copy-done | bytes 262168
  24.1 12.5 %synth.1 = bf16[16,56,128]{2,1,0:T(8,128)(2,1)} custom-call(s32[2]{0:T(128)} %modes.1, bf16[2,2,96,4096]{3,2,1,0:T(8,128)(2,1)} %reshape.14.coef, bf16[8,2,2,4096]{3,2,1,0:T(2,128)(2,1)} %copy-done, bf16[2,2,4096,256]{3,2,1,0:T(8,128)(2,1)} %table.1, f32[16,4,8,512]{3,2,1,0:T(8,128)} %reshape.16.weights), custom_call_target="tpu_custom_call" | custom-call | tf_op jit(solution)/shard_map/synth/pallas_call | solution.py:100
  36.7 28.9 %all_to_all.10.got = bf16[16,56,128]{2,1,0:T(8,128)(2,1)} all-to-all(bf16[16,56,128]{2,1,0:T(8,128)(2,1)} %synth.1), channel_id=1, replica_groups=mesh['blk'=16,'beam'=8] {'blk'}, dimensions={0} | all-to-all | bytes 458752 | tf_op jit(solution)/shard_map/all_to_all | solution.py:167
  65.5 2.2 %to_map.1 = bf16[16,3,32,128]{3,2,1,0:T(8,128)(2,1)} custom-call(bf16[16,56,128]{2,1,0:T(8,128)(2,1)} %all_to_all.10.got), custom_call_target="tpu_custom_call" | custom-call | tf_op jit(solution)/shard_map/to_map/pallas_call | solution.py:145
Async XLA Ops:
  1.7 21.7 %all-to-all-start = ((bf16[8,2,2,4096]{3,2,1,0:T(2,128)(2,1)}), bf16[8,2,2,4096]{3,2,1,0:T(2,128)(2,1)S(1)}, u32[]{:S(2)}, u32[]{:S(2)}) async-start(bf16[8,2,2,4096]{3,2,1,0:T(2,128)(2,1)} %broadcast_in_dim.6), calls=%async_computation | async-start | bytes 524288 | tf_op jit(solution)/shard_map/all_to_all | solution.py:158
  7.5 5.0 %copy-start.1 = (f32[16,16,512]{2,1,0:T(8,128)S(1)}, f32[16,16,512]{2,1,0:T(8,128)}, u32[]{:S(2)}) copy-start(f32[16,16,512]{2,1,0:T(8,128)} %param.9) | copy-start | bytes 1572868
  23.4 0.7 %copy-start = (bf16[8,2,2,4096]{3,2,1,0:T(2,128)(2,1)}, bf16[8,2,2,4096]{3,2,1,0:T(2,128)(2,1)S(1)}, u32[]{:S(2)}) copy-start(bf16[8,2,2,4096]{3,2,1,0:T(2,128)(2,1)S(1)} %all-to-all-done.window) | copy-start | bytes 786436

commit v2 on v1

v2 whole, which is shorter than its diff:
```python
import math

import jax
import jax.numpy as jnp
from jax import lax
from jax.experimental import pallas as pl
from jax.experimental.pallas import tpu as pltpu
from jax.sharding import PartitionSpec as P

LMAX = 8192
NPHI = 128
CHUNK = 1024
TILES = CHUNK // 128
BLOCK = 16
BF = jnp.bfloat16
F32 = jnp.float32


def mirror():
    lane = lax.broadcasted_iota(jnp.int32, (256, 256), 0)
    return jnp.where(lane + lax.broadcasted_iota(jnp.int32, (256, 256), 1) == 255, 1.0, 0.0).astype(BF)


def arrange_kernel(me, sky, orient, coef, weights, wide, lines):
    del me
    wide[...] = sky[...].astype(F32).reshape(wide.shape)
    for cr in range(6):
        for row in range(BLOCK):
            line = wide[pl.ds(cr * BLOCK + row, 16, stride=6 * BLOCK), :].astype(BF)
            coef[row % 2, 0, pl.ds(cr * 16, 16), pl.ds(row // 2 * 128, 128)] = line

    @pl.when((pl.program_id(0) == 0) & (pl.program_id(1) == 0))
    def _():
        flip = mirror()
        for t in range(4):
            lines[pl.ds(256 * t, 256), :] = orient[:, pl.ds(128 * t, 128)]

        def pick(k, t):
            return lines[pl.ds(256 * t + k, 16, stride=16), :]

        for k in range(16):
            weights[k, :, pl.ds(0, 256)] = jnp.concatenate([pick(k, 0), pick(k, 1)], 1)
        south = jnp.concatenate([jnp.concatenate([pick(k, 2), pick(k, 3)], 1) for k in range(16)], 0)
        total = jnp.zeros((256, 256), F32)
        for _ in range(3):
            piece = south.astype(BF)
            total = total + jnp.dot(piece, flip, preferred_element_type=F32)
            south = south - piece.astype(F32)
        weights[:, :, pl.ds(256, 256)] = total.reshape(16, 16, 256)


def arrange(me, sky, orient):
    half = sky.shape[4] // 2 * 128
    steps = sky.shape[4] // BLOCK
    lanes = BLOCK // 2 * 128
    return pl.pallas_call(
        arrange_kernel,
        out_shape=(
            jax.ShapeDtypeStruct((2, 2, 96, half), BF),
            jax.ShapeDtypeStruct((16, 16, 512), F32),
        ),
        grid_spec=pltpu.PrefetchScalarGridSpec(
            num_scalar_prefetch=1,
            grid=(2, steps),
            in_specs=[
                pl.BlockSpec((1, 16, 3, 2, BLOCK, 128), lambda p, i, me: (p, me[0], 0, 0, i, 0)),
                pl.BlockSpec((256, 512), lambda p, i, me: (0, 0)),
            ],
            out_specs=[
                pl.BlockSpec((2, 1, 96, lanes), lambda p, i, me: (0, p, 0, i)),
                pl.BlockSpec((16, 16, 512), lambda p, i, me: (0, 0, 0)),
            ],
            scratch_shapes=[pltpu.VMEM((96 * BLOCK, 128), F32), pltpu.VMEM((1024, 128), F32)],
        ),
        cost_estimate=pl.CostEstimate(flops=10**8, bytes_accessed=8 * 10**6, transcendentals=0),
        name="arrange",
    )(me, sky, orient)


def synth_kernel(modes, coef, window, table, weights, out, sky, leg, acc, win, sems, coef_sems):
    half = leg.shape[2]
    chunks = half // CHUNK

    def first(slot, p):
        return jnp.minimum((modes[slot] - p + 1) // 2 // CHUNK, chunks - 1)

    def place(c):
        return pl.ds(pl.multiple_of(c * CHUNK, CHUNK), CHUNK)

    def copies(slot, p, c):
        at = place(c)
        return (
            pltpu.make_async_copy(coef.at[slot, p, :, at], sky.at[slot, p, :, at], coef_sems.at[slot, p, c]),
            pltpu.make_async_copy(table.at[slot, p, at, :], leg.at[slot, p, at, :], sems.at[slot, p, c]),
        )

    def begin(slot, p, c):
        for copy in copies(slot, p, c):
            copy.start()

    def finish(slot, p, c):
        for copy in copies(slot, p, c):
            copy.wait()

    for slot in range(2):
        for p in range(2):
            lax.fori_loop(first(slot, p), chunks, lambda c, _: (begin(slot, p, c), 0)[1], 0)

    win[...] = window[...].astype(F32).reshape(win.shape)

    def step(slot, p, c):
        finish(slot, p, c)
        at = place(c)
        lines = [sky[slot, p, pl.ds(16 * j, 16), at] for j in range(6)]
        parts = []
        for k in range(16):
            base = (k // 2 * 2 + p) * (half // 64) + k % 2 + c * (2 * TILES)
            gain = jnp.concatenate(
                [jnp.broadcast_to(win[pl.ds(base + 2 * i, 1), :], (16, 128)).astype(BF) for i in range(TILES)], 1
            )
            parts += [line * gain for line in lines]
        return jnp.dot(jnp.concatenate(parts, 0), leg[slot, p, at, :], preferred_element_type=F32)

    flip = mirror()
    to_row = lax.broadcasted_iota(jnp.int32, (96, 96), 0)
    from_row = lax.broadcasted_iota(jnp.int32, (96, 96), 1)
    wanted = to_row % 24 // 4 * 16 + to_row % 4 * 4 + to_row // 24
    order = jnp.where(from_row == wanted, 1.0, 0.0).astype(BF)
    group = lax.broadcasted_iota(jnp.int32, (24, 128), 1) // 32
    for slot in range(2):
        for p in range(2):
            acc[p] = jnp.zeros(acc.shape[1:], F32)

            def body(c, _, slot=slot, p=p):
                part = step(slot, p, c)
                acc[p] = acc[p] + part
                return 0

            lax.fori_loop(first(slot, p), chunks, body, 0)
        sign = jnp.where(modes[slot] % 2 == 0, 1.0, -1.0).astype(F32)
        north, south = [], []
        for cr in range(6):
            for h in range(2):
                n = jnp.zeros((8, 256), F32)
                s = jnp.zeros((8, 256), F32)
                for k in range(16):
                    at = pl.ds(k * 96 + cr * 16 + h * 8, 8)
                    even, odd = acc[0, at, :], acc[1, at, :]
                    n = n + (even + odd) * weights[k, pl.ds(h * 8, 8), pl.ds(0, 256)]
                    s = s + (even - odd) * weights[k, pl.ds(h * 8, 8), pl.ds(256, 256)]
                north.append(n)
                south.append(s * sign)
        north = jnp.concatenate(north, 0).astype(BF)
        south = jnp.dot(jnp.concatenate(south, 0).astype(BF), flip, preferred_element_type=F32).astype(BF)
        both = jnp.dot(order, jnp.concatenate([north, south], 1), preferred_element_type=F32)
        for tile in range(4):
            part = both[:, tile * 128:(tile + 1) * 128]
            for g in range(4):
                send = jnp.zeros((24, 128), F32)
                for b in range(4):
                    piece = part[b * 24:(b + 1) * 24]
                    if b != g:
                        piece = pltpu.roll(piece, ((b - g) * 32) % 128, 1)
                    send = jnp.where(group == b, piece, send)
                out[tile * 4 + g, pl.ds(slot * 24, 24), :] = send.astype(BF)
    sub = lax.broadcasted_iota(jnp.int32, (8, 128), 0)
    tail = jnp.zeros((8, 128), jnp.int32)
    for slot in range(2):
        tail = jnp.where(sub == 2 * slot, modes[slot] // 128, tail)
        tail = jnp.where(sub == 2 * slot + 1, modes[slot] % 128, tail)
    tail = tail.astype(F32).astype(BF)
    for dst in range(16):
        out[dst, pl.ds(48, 8), :] = tail


def synth(modes, coef, window, table, weights):
    half = coef.shape[3]
    chunks = half // CHUNK
    vm = pl.BlockSpec(memory_space=pltpu.VMEM)
    hbm = pl.BlockSpec(memory_space=pl.ANY)
    return pl.pallas_call(
        synth_kernel,
        out_shape=jax.ShapeDtypeStruct((16, 56, 128), BF),
        in_specs=[pl.BlockSpec(memory_space=pltpu.SMEM), hbm, vm, hbm, vm],
        out_specs=vm,
        scratch_shapes=[
            pltpu.VMEM((2, 2, 96, half), BF),
            pltpu.VMEM((2, 2, half, 256), BF),
            pltpu.VMEM((2, 1536, 256), F32),
            pltpu.VMEM((window.shape[0] * 2 * half // 64, 128), F32),
            pltpu.SemaphoreType.DMA((2, 2, chunks)),
            pltpu.SemaphoreType.DMA((2, 2, chunks)),
        ],
        cost_estimate=pl.CostEstimate(flops=13 * 10**9, bytes_accessed=12 * 10**6, transcendentals=0),
        name="synth",
    )(modes, coef, window, table, weights)


def map_kernel(got, out, wide):
    wide[...] = got[...].reshape(wide.shape).astype(F32)

    def take(row):
        return wide[pl.ds(row, 16, stride=56), :]

    column = lax.broadcasted_iota(jnp.int32, (16, 128), 1)
    cosines, sines = [], []
    for slot in range(2):
        mode = (take(48 + 2 * slot) * 128.0 + take(49 + 2 * slot)).astype(jnp.int32)
        phase = ((mode * column) % (2 * LMAX)).astype(F32) * (math.pi / LMAX)
        weight = jnp.where(mode == 0, 1.0, 2.0)
        cosines.append(weight * jnp.cos(phase))
        sines.append(-weight * jnp.sin(phase))
    basis = jnp.concatenate(cosines + sines, 0)
    high = basis.astype(BF)
    low = (basis - high.astype(F32)).astype(BF)
    basis = jnp.concatenate([high, low], 0)
    for c in range(3):
        for a in range(4):
            x = jnp.concatenate([take(slot * 24 + c * 8 + r * 4 + a) for r in range(2) for slot in range(2)], 0)
            x = x.T.astype(BF)
            y = jnp.dot(jnp.concatenate([x, x], 1), basis, preferred_element_type=F32)
            for b in range(4):
                out[4 * a + b, c] = y[b * 32:(b + 1) * 32].astype(BF)


def to_map(got):
    vm = pl.BlockSpec(memory_space=pltpu.VMEM)
    return pl.pallas_call(
        map_kernel,
        out_shape=jax.ShapeDtypeStruct((16, 3, 32, NPHI), BF),
        in_specs=[vm],
        out_specs=vm,
        scratch_shapes=[pltpu.VMEM((16 * 56, 128), F32)],
        name="to_map",
    )(got)


def paired(x):
    lead = x.shape[:-2]
    x = x.reshape(lead + (2, x.shape[-1] // 128, 128))
    return jnp.swapaxes(x, -3, -2).reshape(lead + (-1, 128))


def shards(sky_coefficients, beam_window, legendre, azimuth_modes, orientation):
    me = lax.axis_index("beam").astype(jnp.int32)[None]
    window = paired(beam_window)
    window = lax.all_to_all(jnp.broadcast_to(window[None], (8,) + window.shape), "beam", 0, 0, tiled=True)
    coef, weights = arrange(me, paired(sky_coefficients), orientation.reshape(256, 512))
    sent = synth(azimuth_modes, coef, window, legendre, weights)
    got = lax.all_to_all(sent, "blk", 0, 0, tiled=True)
    return to_map(got)


def solution(mesh):
    placed = (
        P(None, None, None, None, "blk", None),
        P(None, "beam", None),
        P("blk", None, None, None),
        P("blk"),
        P("beam", None, None),
    )
    return jax.shard_map(
        shards, mesh=mesh, in_specs=placed, out_specs=P("beam", None, "blk", None), check_vma=False
    )
```

time: 67.9 us -> 54.6 us (0.80)
  local copies, waits for them, and re-layouts: 17.2 us -> 2.27 us
  Pallas kernels: 14.8 us -> 26.1 us
  blocking collectives: 28.9 us -> 19.9 us
  other arithmetic: 1 us -> 0 us
    all_to_all x1, blocking collectives: 28.9 us -> 19.9 us  [shards(): got = lax.all_to_all(sent, 'blk', 0, 0, tiled=True)]
    pallas_call x0 -> x1, Pallas kernels: none -> 8.71 us  [arrange(): pl.pallas_call(arrange_kernel, out_shape=(jax.ShapeDtypeStruct((2, 2, 96,...]
    dynamic_slice x1 -> x0, local copies, waits for them, and re-layouts: 5 us -> none  [shards(): coef = lax.dynamic_slice_in_dim(sky_coefficients, me * 16, 16, 1)]
    reshape x2 -> x1, local copies, waits for them, and re-layouts: 4.34 us -> 0.79 us  [paired(): x = x.reshape(lead + (2, x.shape[-1] // 128, 128))]
    transpose x1, local copies, waits for them, and re-layouts: 3.04 us -> 0.03 us  [paired(): return jnp.swapaxes(x, -3, -2).reshape(lead + (-1, 128))]
    pallas_call x1, Pallas kernels: 12.5 us -> 15.1 us  [synth(): pl.pallas_call(synth_kernel, out_shape=jax.ShapeDtypeStruct((16, 56, 128)...]
    broadcast_in_dim x3 -> x1, local copies, waits for them, and re-layouts: 2.19 us -> 0.75 us  [shards(): jnp.broadcast_to(window[None], (8,) + window.shape)]
    rev x1 -> x0, local copies, waits for them, and re-layouts: 1.12 us -> none  [shards(): jnp.flip(weights[..., 256:], -1)]
  transfers between devices with their start and end apart: 1 -> 1, of which waited for: 0 -> 0; matrix products, arithmetic and copies ran while one was open for 23% -> 0% of each run, Pallas kernels for 0% -> 16%
where the time goes in v2:
time: 54.6 us; the launch traced here: 54.1 us
  Pallas kernels  26.1 us (48%)
  blocking collectives  19.9 us (36%)
  starting transfers between devices  5.79 us (11%)
  local copies, waits for them, and re-layouts  2.27 us (4%)
    all_to_all x1, blocking collectives, shards(): got = lax.all_to_all(sent, 'blk', 0, 0, tiled=True)  19.9 us
    pallas_call x1, Pallas kernels, synth(): pl.pallas_call(synth_kernel, out_shape=jax.ShapeDtypeStruct((16, 56, 128)...  15.1 us
    pallas_call x1, Pallas kernels, arrange(): pl.pallas_call(arrange_kernel, out_shape=(jax.ShapeDtypeStruct((2, 2, 96,...  8.71 us
    all_to_all x1, starting transfers between devices, shards(): lax.all_to_all(jnp.broadcast_to(window[None], (8,) + window.shape), 'beam...  5.79 us
    pallas_call x1, Pallas kernels, to_map(): pl.pallas_call(map_kernel, out_shape=jax.ShapeDtypeStruct((16, 3, 32, NPH...  2.24 us
  transfers between devices with their start and end apart: 1, of which 0 were waited for; matrix products, arithmetic and copies ran while one was open for 0% of the time, Pallas kernels for 16%

profile of v2, /device:TPU:1, one launch (start us, length us, event | category | flops | bytes accessed | tf_op | source)
XLA Modules:
  0.0 54.1 jit_solution(7527329637086836593)
XLA Ops:
  0.0 0.8 %reshape.16 = bf16[2,2,32,128]{3,2,1,0:T(8,128)(2,1)S(1)} reshape(bf16[2,2,4096]{2,1,0:T(2,128)(2,1)} %param.6) | data formatting | bytes 65536 | tf_op jit(solution)/shard_map/reshape | solution.py:240
  0.8 0.8 %broadcast_in_dim.12 = bf16[8,2,64,128]{3,2,1,0:T(8,128)(2,1)} broadcast(bf16[2,64,128]{2,1,0:T(8,128)(2,1)S(1)} %bitcast.11), dimensions={1,2,3} | broadcast | bytes 294912 | tf_op jit(solution)/shard_map/broadcast_in_dim | solution.py:247
  1.6 5.8 %all-to-all-start = ((bf16[8,2,64,128]{3,2,1,0:T(8,128)(2,1)}), bf16[8,2,64,128]{3,2,1,0:T(8,128)(2,1)S(1)}, u32[]{:S(2)}, u32[]{:S(2)}) async-start(bf16[8,2,64,128]{3,2,1,0:T(8,128)(2,1)} %broadcast_in_dim.12), calls=%async_computation | async-start | bytes 524288 | tf_op jit(solution)/shard_map/all_to_all | solution.py:247
  7.4 8.7 %arrange.1 = (bf16[2,2,96,4096]{3,2,1,0:T(8,128)(2,1)}, f32[16,16,512]{2,1,0:T(8,128)}) custom-call(s32[1]{0:T(128)} %bitcast.me, bf16[2,128,3,2,64,128]{5,4,3,2,1,0:T(8,128)(2,1)} %bitcast.9, f32[256,512]{1,0:T(8,128)} %bitcast.10), custom_call_target="tpu_custom_call" | custom-call | flops 100000000 | bytes 8000000 | tf_op jit(solution)/shard_map/arrange/pallas_call | solution.py:56
  16.1 0.0 all-to-all-done.window
  16.1 0.0 copy-start
  16.1 0.7 %copy-done = bf16[8,2,64,128]{3,2,1,0:T(8,128)(2,1)} copy-done((bf16[8,2,64,128]{3,2,1,0:T(8,128)(2,1)}, bf16[8,2,64,128]{3,2,1,0:T(8,128)(2,1)S(1)}, u32[]{:S(2)}) %copy-start) | copy-done | bytes 262168
  16.8 15.1 %synth.1 = bf16[16,56,128]{2,1,0:T(8,128)(2,1)} custom-call(s32[2]{0:T(128)} %modes.1, bf16[2,2,96,4096]{3,2,1,0:T(8,128)(2,1)} %get-tuple-element.7.coef, bf16[8,2,64,128]{3,2,1,0:T(8,128)(2,1)} %copy-done, bf16[2,2,4096,256]{3,2,1,0:T(8,128)(2,1)} %table.1, f32[16,16,512]{2,1,0:T(8,128)} %get-tuple-element.8.weights), custom_call_target="tpu_custom_call" | custom-call | flops 12999999488 | bytes 12000000 | tf_op jit(solution)/shard_map/synth/pallas_call | solution.py:181
  31.9 19.9 %all_to_all.10.got = bf16[16,56,128]{2,1,0:T(8,128)(2,1)} all-to-all(bf16[16,56,128]{2,1,0:T(8,128)(2,1)} %synth.1), channel_id=1, replica_groups=mesh['blk'=16,'beam'=8] {'blk'}, dimensions={0} | all-to-all | bytes 458752 | tf_op jit(solution)/shard_map/all_to_all | solution.py:250
  51.8 2.2 %to_map.1 = bf16[16,3,32,128]{3,2,1,0:T(8,128)(2,1)} custom-call(bf16[16,56,128]{2,1,0:T(8,128)(2,1)} %all_to_all.10.got), custom_call_target="tpu_custom_call" | custom-call | tf_op jit(solution)/shard_map/to_map/pallas_call | solution.py:228
  (1 shorter events, 0.0 us)
Async XLA Ops:
  1.6 14.5 %all-to-all-start = ((bf16[8,2,64,128]{3,2,1,0:T(8,128)(2,1)}), bf16[8,2,64,128]{3,2,1,0:T(8,128)(2,1)S(1)}, u32[]{:S(2)}, u32[]{:S(2)}) async-start(bf16[8,2,64,128]{3,2,1,0:T(8,128)(2,1)} %broadcast_in_dim.12), calls=%async_computation | async-start | bytes 524288 | tf_op jit(solution)/shard_map/all_to_all | solution.py:247
  16.1 0.7 %copy-start = (bf16[8,2,64,128]{3,2,1,0:T(8,128)(2,1)}, bf16[8,2,64,128]{3,2,1,0:T(8,128)(2,1)S(1)}, u32[]{:S(2)}) copy-start(bf16[8,2,64,128]{3,2,1,0:T(8,128)(2,1)S(1)} %all-to-all-done.window) | copy-start | bytes 786436
